TPU v7x, 512 devices: a whole 4x8x8 slice. The times are simulated.
512 devices in a mesh: ctx: 64 (over x, z, core), head: 8 (over y).
Axes of the slice: x: 4, y: 8, z: 8, core: 2. Of those that a mesh axis runs over, the one named last changes fastest.
Arguments:
- dec_states: bfloat16 [16384, 4096], P('ctx', 'head'), may hold values from -512 to 512
- norm_gain: float32 [4096], replicated, may hold values from 0.1 to 1.9
- w_query: bfloat16 [4096, 4096], P('ctx', 'head'), may hold values from -0.09375 to 0.09375
- enc_keys: bfloat16 [131072, 4096], P('ctx', 'head'), may hold values from -128 to 128
- enc_values: bfloat16 [131072, 4096], P('ctx', 'head'), may hold values from -24 to 24
- w_out: bfloat16 [4096, 4096], P('ctx', 'head'), may hold values from -0.09375 to 0.09375
- tgt_lengths: int32 [32], replicated, may hold values from 1 to 512, 8192 in all
- src_lengths: int32 [32], replicated, may hold values from 2049 to 4096, as said below
Outputs:
- attn_output: bfloat16 [16384, 4096], P('ctx', 'head')
Inputs may be any that keep to these rules, and one draw needn't show every extreme that they name: `tgt_lengths`: the lengths sum to 8192, and the longest equals 512. `src_lengths`: every example has more than 2048 encoder rows, and some example has all 4096.
All inputs are finite; a program needn't handle non-finite values.
Results may differ from a plain program's by a relative error of at most 0.009.
Values may be sent and summed in bfloat16 or wider, within the bound.
No kernel may reach another device: no remote copies, remote signals or barrier semaphores. Data moves between devices by JAX's collectives and lax.ppermute only.
A program may use at most 64 MiB of HBM per device.

v0:
```python
import jax
import jax.numpy as jnp
from jax import lax
from jax.sharding import PartitionSpec as P

DK = 64


def partner(value, axis, distance):
    mask = 2**distance
    pairs = [(source, source ^ mask) for source in range(lax.axis_size(axis))]
    return lax.ppermute(value, axis, pairs)


def attend(queries, keys, values, key_valid):
    row_count = queries.shape[0]
    head_count = queries.shape[1] // DK
    query_heads = jnp.moveaxis(queries.reshape(row_count, head_count, DK), 1, 0)
    key_heads = jnp.moveaxis(keys.reshape(-1, head_count, DK), 1, 0)
    value_heads = jnp.moveaxis(values.reshape(-1, head_count, DK), 1, 0)

    def one_head(head_items):
        query_head, key_head, value_head = head_items
        scores = jnp.dot(query_head, key_head.T, preferred_element_type=jnp.float32)
        scores = jnp.where(key_valid[None, :], scores, -jnp.inf)
        top_score = jnp.max(scores, axis=1)
        weights = jnp.exp(scores - top_score[:, None]).astype(jnp.bfloat16)
        totals = jnp.sum(weights.astype(jnp.float32), axis=1)
        weighted = jnp.dot(weights, value_head, preferred_element_type=jnp.float32)
        return (top_score, totals, weighted)

    top_score, totals, weighted = lax.map(one_head, (query_heads, key_heads, value_heads))
    return (top_score.T, totals.T, jnp.moveaxis(weighted, 0, 1).reshape(row_count, head_count * DK))


def combine_halves(first, second):
    top_one, totals_one, weighted_one = first
    top_two, totals_two, weighted_two = second
    row_count = weighted_one.shape[0]
    head_count = top_one.shape[1]
    largest = jnp.maximum(top_one, top_two)
    scale_one = jnp.exp(top_one - largest)
    scale_two = jnp.exp(top_two - largest)
    numer = (
        weighted_one.reshape(row_count, head_count, DK) * scale_one[:, :, None]
        + weighted_two.reshape(row_count, head_count, DK) * scale_two[:, :, None]
    )
    denom = totals_one * scale_one + totals_two * scale_two
    return (numer / denom[:, :, None]).reshape(row_count, head_count * DK)


def local(dec_states, norm_gain, w_query, enc_keys, enc_values, w_out, tgt_lengths, src_lengths):
    position = lax.axis_index("ctx")
    half_index = position % 2
    example = position // 2
    slot_ids = jnp.arange(tgt_lengths.shape[0], dtype=jnp.int32)
    tgt_len = jnp.sum(jnp.where(slot_ids == example, tgt_lengths, 0))
    src_len = jnp.sum(jnp.where(slot_ids == example, src_lengths, 0))
    enc_count = enc_keys.shape[0]
    full_states = lax.all_gather(dec_states, "head", axis=1, tiled=True)
    row_count = full_states.shape[0]
    states = full_states.astype(jnp.float32)
    normed = (
        states * lax.rsqrt(jnp.mean(states * states, axis=-1, keepdims=True) + 1e-06) * norm_gain
    ).astype(jnp.bfloat16)
    columns = normed
    queries = jnp.dot(
        columns,
        lax.all_gather(w_query, "ctx", axis=0, tiled=True),
        preferred_element_type=jnp.float32,
    ).astype(jnp.bfloat16)
    offsets = jnp.arange(enc_count, dtype=jnp.int32)
    own_valid = half_index * enc_count + offsets < src_len
    far_valid = (1 - half_index) * enc_count + offsets < src_len
    far_keys, far_values = partner((enc_keys, enc_values), "ctx", 0)
    nearby = attend(queries, enc_keys, enc_values, own_valid)
    distant = attend(queries, far_keys, far_values, far_valid)
    attended = combine_halves(nearby, distant)
    live_rows = half_index * row_count + jnp.arange(row_count, dtype=jnp.int32) < tgt_len
    attended = jnp.where(live_rows[:, None], attended, 0.0).astype(jnp.bfloat16)
    all_heads = lax.all_gather(attended, "head", axis=1, tiled=True)
    columns = all_heads
    projected = jnp.dot(
        columns,
        lax.all_gather(w_out, "ctx", axis=0, tiled=True),
        preferred_element_type=jnp.float32,
    )
    return projected.astype(jnp.bfloat16)


def solution(mesh):
    placed = (
        P("ctx", "head"),
        P(),
        P("ctx", "head"),
        P("ctx", "head"),
        P("ctx", "head"),
        P("ctx", "head"),
        P(),
        P(),
    )
    return jax.shard_map(
        local, mesh=mesh, in_specs=placed, out_specs=P("ctx", "head"), check_vma=False
    )
```

profile of v0, /device:TPU:2, one launch (start us, length us, event | category | flops | bytes accessed | tf_op | source)
XLA Modules:
  0.0 284.5 jit_solution(14177036345322470178)
XLA Ops:
  6.5 0.7 all-gather.5.cloned.1.call-update
  7.3 0.7 all-gather.7.cloned.1.call-update
  8.1 2.9 %copy.11 = bf16[2048,512]{0,1:T(8,128)(2,1)S(1)} copy(bf16[2048,512]{1,0:T(8,128)(2,1)} %param.15) | data formatting | bytes 4194304 | tf_op args[3]
  11.0 1.9 collective-permute-start
  12.9 4.0 %copy.12 = bf16[2048,512]{0,1:T(8,128)(2,1)} copy(bf16[2048,512]{1,0:T(8,128)(2,1)} %param.16) | data formatting | bytes 4194304 | tf_op args[4]
  16.9 2.5 collective-permute-start.1
  19.6 0.6 fusion.38
  20.2 0.6 add_compare_fusion.2
  20.8 0.6 fusion.39
  21.5 36.2 %all-gather.5.cloned.1.call-done = bf16[256,4096]{1,0:T(8,128)(2,1)} async-done(((bf16[256,512]{1,0:T(8,128)(2,1)}), bf16[256,4096]{1,0:T(8,128)(2,1)}) %all-gather.5.cloned.1.call-update) | async-done | bytes 2097168 | tf_op jit(solution)/shard_map/all_gather | solution.py:60
  57.7 2.1 fusion.22
  59.8 84.6 %all-gather.7.cloned.1.call-done = bf16[4096,512]{1,0:T(8,128)(2,1)} async-done(((bf16[64,512]{1,0:T(8,128)(2,1)}), bf16[4096,512]{1,0:T(8,128)(2,1)}) %all-gather.7.cloned.1.call-update) | async-done | bytes 4194320 | tf_op jit(solution)/shard_map/all_gather | solution.py:69
  144.4 4.1 %fusion.29 = bf16[256,512]{1,0:T(8,128)(2,1)S(1)} fusion(bf16[4096,512]{1,0:T(8,128)(2,1)} %all-gather.7.cloned.1.call-done, bf16[256,4096]{1,0:T(8,128)(2,1)} %all-gather.5.cloned.1.call-done, f32[4096]{0:T(1024)S(1)} %copy-done.1, f32[256]{0:T(256)S(1)} %add_rsqrt_fusion), kind=kOutput, calls=%fused_computation.38 | convolution fusion | flops 1078067200 | bytes 6571008 | tf_op jit(solution)/shard_map/dot_general | solution.py:67
  149.0 32.8 %while.31 = (s32[]{:T(128)}, f32[8,256]{1,0:T(8,128)S(1)}, f32[8,256]{1,0:T(8,128)S(1)}, f32[8,256,64]{1,2,0:T(8,128)S(1)}, bf16[8,256,64]{2,1,0:T(8,128)(2,1)S(...) while((s32[]{:T(128)}, f32[8,256]{1,0:T(8,128)S(1)}, ...), condition=%wide.region_10.11_spmd.clone, body=%wide.region_7.10_spmd.clone.sunk | while | flops 138415616 | bytes 6961277 | solution.py:32
  149.0 0.6 add_compare_fusion.6
  149.6 1.4 fusion.57
  151.1 1.5 fusion.58
  153.1 0.6 add_compare_fusion.6
  153.7 1.4 fusion.57
  155.2 1.5 fusion.58
  157.2 0.6 add_compare_fusion.6
  157.8 1.5 fusion.57
  159.3 1.5 fusion.58
  161.3 0.6 add_compare_fusion.6
  161.9 1.4 fusion.57
  163.4 1.5 fusion.58
  165.4 0.6 add_compare_fusion.6
  166.0 1.4 fusion.57
  167.5 1.5 fusion.58
  169.5 0.6 add_compare_fusion.6
  170.1 1.4 fusion.57
  171.6 1.5 fusion.58
  173.6 0.6 add_compare_fusion.6
  174.2 1.4 fusion.57
  175.7 1.5 fusion.58
  177.7 0.6 add_compare_fusion.6
  178.3 1.4 fusion.57
  179.8 1.5 fusion.58
  181.8 0.8 copy-done
  182.6 25.2 %while.30 = (s32[]{:T(128)}, f32[8,256]{1,0:T(8,128)S(1)}, f32[8,256]{1,0:T(8,128)S(1)}, f32[8,256,64]{1,2,0:T(8,128)S(1)}, bf16[8,256,64]{2,1,0:T(8,128)(2,1)S(...) while((s32[]{:T(128)}, f32[8,256]{1,0:T(8,128)S(1)}, ...), condition=%wide.region_6.7_spmd.clone, body=%wide.region_3.6_spmd.clone.sunk | while | flops 138415616 | bytes 6961277 | solution.py:32
  182.6 0.6 add_compare_fusion.5
  183.8 1.5 fusion.55
  185.8 0.6 add_compare_fusion.5
  186.4 0.5 fusion.54
  186.9 1.5 fusion.55
  188.9 0.6 add_compare_fusion.5
  190.1 1.5 fusion.55
  192.1 0.6 add_compare_fusion.5
  193.2 1.5 fusion.55
  195.2 0.6 add_compare_fusion.5
  195.9 0.5 fusion.54
  196.4 1.5 fusion.55
  198.4 0.6 add_compare_fusion.5
  199.0 0.5 fusion.54
  199.5 1.5 fusion.55
  201.6 0.6 add_compare_fusion.5
  202.7 1.5 fusion.55
  204.7 0.6 add_compare_fusion.5
  205.8 1.5 fusion.55
  207.9 1.1 fusion.34
  209.0 0.8 fusion.32
  209.8 19.9 %all-gather.11.cloned.1.call-done = bf16[4096,512]{1,0:T(8,128)(2,1)} async-done(((bf16[64,512]{1,0:T(8,128)(2,1)}), bf16[4096,512]{1,0:T(8,128)(2,1)}) %all-gather.11.cloned.1.call-update) | async-done | bytes 4194320 | tf_op jit(solution)/shard_map/all_gather | solution.py:85
  229.7 43.5 %all-gather.9.cloned.1.call-done = bf16[256,4096]{0,1:T(8,128)(2,1)} async-done(((bf16[256,512]{0,1:T(8,128)(2,1)}), bf16[256,4096]{0,1:T(8,128)(2,1)}) %all-gather.9.cloned.1.call-update) | async-done | bytes 2097168 | tf_op jit(solution)/shard_map/all_gather | solution.py:81
  273.1 4.8 %convolution_convert_fusion = bf16[256,512]{1,0:T(8,128)(2,1)} fusion(bf16[256,4096]{0,1:T(8,128)(2,1)} %all-gather.9.cloned.1.call-done, bf16[4096,512]{1,0:T(8,128)(2,1)} %all-gather.11.cloned.1.call-done), kind=kOutput, calls=%fused_computation.39 | convolution fusion | flops 1073872896 | bytes 6553600 | tf_op jit(solution)/shard_map/dot_general | solution.py:83
  (78 shorter events, 11.5 us)
Async XLA Ops:
  6.5 51.2 %all-gather.5.cloned.1.call-start = ((), (), s32[]{:S(2)}) async-start(), calls=%async_computation | async-start | bytes 2359296 | tf_op jit(solution)/shard_map/all_gather | solution.py:60
  7.3 137.1 %all-gather.7.cloned.1.call-start = ((), (), s32[]{:S(2)}) async-start(), calls=%async_computation.1 | async-start | bytes 4259840 | tf_op jit(solution)/shard_map/all_gather | solution.py:69
  8.0 221.6 %all-gather.11.cloned.1.call-start = ((), (), s32[]{:S(2)}) async-start(), calls=%async_computation.3 | async-start | bytes 4259840 | tf_op jit(solution)/shard_map/all_gather | solution.py:85
  11.0 8.6 %copy-start.2 = (s32[32]{0:T(128)S(1)}, s32[32]{0:T(128)}, u32[]{:S(2)}) copy-start(s32[32]{0:T(128)} %param.18) | copy-start | bytes 388
  11.0 9.8 %copy-start.3 = (s32[32]{0:T(128)S(1)}, s32[32]{0:T(128)}, u32[]{:S(2)}) copy-start(s32[32]{0:T(128)} %param.19) | copy-start | bytes 388
  11.0 137.9 %collective-permute-start = (bf16[2048,512]{0,1:T(8,128)(2,1)S(1)}, bf16[2048,512]{0,1:T(8,128)(2,1)}, u32[]{:S(2)}, u32[]{:S(2)}) collective-permute-start(bf16[2048,512]{0,1:T(8,128)(2,1)S(1)} %copy.11), channel_id=1, source_target_pairs={{0,8},{8,0},{16,24},{24,16},{32,40},{40,32},{48,56},{56,48},{64,72... | collective-permute-start | bytes 6291464 | tf_op jit(solution)/shard_map/ppermute | solution.py:12
  16.9 127.4 %copy-start.1 = (f32[4096]{0:T(1024)S(1)}, f32[4096]{0:T(1024)}, u32[]{:S(2)}) copy-start(f32[4096]{0:T(1024)} %param.13) | copy-start | bytes 49156
  16.9 132.0 %collective-permute-start.1 = (bf16[2048,512]{0,1:T(8,128)(2,1)}, bf16[2048,512]{0,1:T(8,128)(2,1)}, u32[]{:S(2)}, u32[]{:S(2)}) collective-permute-start(bf16[2048,512]{0,1:T(8,128)(2,1)} %copy.12), channel_id=1, source_target_pairs={{0,8},{8,0},{16,24},{24,16},{32,40},{40,32},{48,56},{56,48},{64,72... | collective-permute-start | bytes 6291464 | tf_op jit(solution)/shard_map/ppermute | solution.py:12
  19.5 253.7 %all-gather.9.cloned.1.call-start = ((), (), s32[]{:S(2)}) async-start(), calls=%async_computation.2 | async-start | bytes 2359296 | tf_op jit(solution)/shard_map/all_gather | solution.py:81
  181.8 0.8 copy-start
Sparse Core Ops, SparseCore 0:
  9.4 48.2 all-gather.4
  61.1 83.2 all-gather.6
  147.7 81.8 all-gather.10
  231.6 41.5 all-gather.8
where the time goes:
time: 286 us; the launch traced here: 284 us
  waiting for transfers between devices  186 us (65%)
  matrix products  48 us (17%)
  other arithmetic  22.9 us (8%)
  between operations  13.3 us (5%)
  local copies, waits for them, and re-layouts  9.49 us (3%)
  starting transfers between devices  4.57 us (2%)
    all_gather x1, waiting for transfers between devices, local(): lax.all_gather(w_query, 'ctx', axis=0, tiled=True)  84.6 us
    all_gather x1, waiting for transfers between devices, local(): all_heads = lax.all_gather(attended, 'head', axis=1, tiled=True)  43.5 us
    all_gather x1, waiting for transfers between devices, local(): full_states = lax.all_gather(dec_states, 'head', axis=1, tiled=True)  36.2 us
    dot_general x16, matrix products, one_head(): weighted = jnp.dot(weights, value_head, preferred_element_type=jnp.float32)  23.5 us
    all_gather x1, waiting for transfers between devices, local(): lax.all_gather(w_out, 'ctx', axis=0, tiled=True)  19.9 us
    dot_general x16, matrix products, one_head(): scores = jnp.dot(query_head, key_head.T, preferred_element_type=jnp.float32)  15.6 us
    unnamed x11, local copies, waits for them, and re-layouts  7.97 us
    reduce_sum x16, other arithmetic, one_head(): totals = jnp.sum(weights.astype(jnp.float32), axis=1)  6.97 us
  transfers between devices with their start and end apart: 6, of which 4 were waited for; matrix products, arithmetic and copies ran while one was open for 26% of the time, Pallas kernels for 0%

commit v1 on v0

--- a/solution.py
+++ b/solution.py
@@ -82,7 +82,9 @@
     columns = all_heads
     projected = jnp.dot(
         columns,
-        lax.all_gather(w_out, "ctx", axis=0, tiled=True),
+        jnp.concatenate(
+            lax.all_to_all(jnp.stack([w_out] * lax.axis_size("ctx")), "ctx", 0, 0), axis=0
+        ),
         preferred_element_type=jnp.float32,
     )
     return projected.astype(jnp.bfloat16)

time: 286 us -> 277 us (0.969)
  waiting for transfers between devices: 186 us -> 156 us
  starting transfers between devices: 4.57 us -> 18.7 us
  matrix products: 48 us -> 55 us
    all_gather x1 -> x0, waiting for transfers between devices: 19.9 us -> none  [local(): lax.all_gather(w_out, 'ctx', axis=0, tiled=True)]
    all_gather x1, waiting for transfers between devices: 36.2 us -> 20 us  [local(): full_states = lax.all_gather(dec_states, 'head', axis=1, tiled=True)]
    all_to_all x0 -> x1, starting transfers between devices: none -> 14.2 us  [local(): lax.all_to_all(jnp.stack([w_out] * lax.axis_size('ctx')), 'ctx', 0, 0)]
    all_gather x1, waiting for transfers between devices: 84.6 us -> 93.1 us  [local(): lax.all_gather(w_query, 'ctx', axis=0, tiled=True)]
    dot_general x16, matrix products: 15.6 us -> 23.1 us  [one_head(): scores = jnp.dot(query_head, key_head.T, preferred_element_type=jnp.float32)]
    unnamed x11 -> x15, local copies, waits for them, and re-layouts: 7.97 us -> 6.91 us
  transfers between devices with their start and end apart: 6 -> 6, of which waited for: 4 -> 3; matrix products, arithmetic and copies ran while one was open for 26% -> 30% of each run, Pallas kernels for 0% -> 0%
where the time goes in v1:
time: 277 us; the launch traced here: 276 us
  waiting for transfers between devices  156 us (56%)
  matrix products  55 us (20%)
  other arithmetic  21.1 us (8%)
  starting transfers between devices  18.7 us (7%)
  between operations  13.3 us (5%)
  local copies, waits for them, and re-layouts  10.9 us (4%)
    all_gather x1, waiting for transfers between devices, local(): lax.all_gather(w_query, 'ctx', axis=0, tiled=True)  93.1 us
    all_gather x1, waiting for transfers between devices, local(): all_heads = lax.all_gather(attended, 'head', axis=1, tiled=True)  41.9 us
    dot_general x16, matrix products, one_head(): weighted = jnp.dot(weights, value_head, preferred_element_type=jnp.float32)  23.5 us
    dot_general x16, matrix products, one_head(): scores = jnp.dot(query_head, key_head.T, preferred_element_type=jnp.float32)  23.1 us
    all_gather x1, waiting for transfers between devices, local(): full_states = lax.all_gather(dec_states, 'head', axis=1, tiled=True)  20 us
    all_to_all x1, starting transfers between devices, local(): lax.all_to_all(jnp.stack([w_out] * lax.axis_size('ctx')), 'ctx', 0, 0)  14.2 us
    reduce_sum x16, other arithmetic, one_head(): totals = jnp.sum(weights.astype(jnp.float32), axis=1)  7.01 us
    unnamed x15, local copies, waits for them, and re-layouts  6.91 us
  transfers between devices with their start and end apart: 6, of which 3 were waited for; matrix products, arithmetic and copies ran while one was open for 30% of the time, Pallas kernels for 0%

profile of v1, /device:TPU:2, one launch (start us, length us, event | category | flops | bytes accessed | tf_op | source)
XLA Modules:
  0.0 276.0 jit_solution(1596267894385225841)
XLA Ops:
  6.5 0.7 all-gather.4.cloned.1.call-update
  7.3 0.7 all-gather.6.cloned.1.call-update
  8.0 4.1 %copy.12 = bf16[2048,512]{0,1:T(8,128)(2,1)} copy(bf16[2048,512]{1,0:T(8,128)(2,1)} %param.16) | data formatting | bytes 4194304 | tf_op args[4]
  12.1 2.0 collective-permute-start.1
  14.2 2.5 copy.11
  16.6 2.4 collective-permute-start
  19.1 2.5 stack.2
  21.5 14.2 %all-to-all-start = ((bf16[64,64,512]{2,1,0:T(8,128)(2,1)}), bf16[64,64,512]{2,1,0:T(8,128)(2,1)}, u32[]{:S(2)}, u32[]{:S(2)}) async-start(bf16[64,64,512]{2,1,0:T(8,128)(2,1)} %stack.2), calls=%async_computation | async-start | bytes 8388608 | tf_op jit(solution)/shard_map/all_to_all | solution.py:86
  35.8 0.6 fusion.38
  37.0 0.6 fusion.39
  37.7 20.0 %all-gather.4.cloned.1.call-done = bf16[256,4096]{1,0:T(8,128)(2,1)} async-done(((bf16[256,512]{1,0:T(8,128)(2,1)}), bf16[256,4096]{1,0:T(8,128)(2,1)}) %all-gather.4.cloned.1.call-update) | async-done | bytes 2097168 | tf_op jit(solution)/shard_map/all_gather | solution.py:60
  57.7 2.2 fusion.22
  59.9 93.1 %all-gather.6.cloned.1.call-done = bf16[4096,512]{1,0:T(8,128)(2,1)} async-done(((bf16[64,512]{1,0:T(8,128)(2,1)}), bf16[4096,512]{1,0:T(8,128)(2,1)}) %all-gather.6.cloned.1.call-update) | async-done | bytes 4194320 | tf_op jit(solution)/shard_map/all_gather | solution.py:69
  153.0 3.5 %fusion.29 = bf16[256,512]{1,0:T(8,128)(2,1)S(1)} fusion(bf16[4096,512]{1,0:T(8,128)(2,1)} %all-gather.6.cloned.1.call-done, bf16[256,4096]{1,0:T(8,128)(2,1)S(1)} %copy-done.1, f32[4096]{0:T(1024)S(1)} %copy-done.3, f32[256]{0:T(256)S(1)} %add_rsqrt_fusion), kind=kOutput, calls=%fused_computation.38 | convolution fusion | flops 1078067200 | bytes 6571008 | tf_op jit(solution)/shard_map/dot_general | solution.py:67
  157.1 32.3 %while.30 = (s32[]{:T(128)}, f32[8,256]{1,0:T(8,128)S(1)}, f32[8,256]{1,0:T(8,128)S(1)}, f32[8,256,64]{1,2,0:T(8,128)S(1)}, bf16[8,256,64]{2,1,0:T(8,128)(2,1)S(...) while((s32[]{:T(128)}, f32[8,256]{1,0:T(8,128)S(1)}, ...), condition=%wide.region_6.7_spmd.clone, body=%wide.region_3.6_spmd.clone.sunk | while | flops 138415616 | bytes 6961285 | solution.py:32
  157.1 0.6 add_compare_fusion.5
  157.7 1.4 fusion.54
  159.6 1.5 fusion.55
  161.1 0.6 add_compare_fusion.5
  161.7 1.4 fusion.54
  163.6 1.5 fusion.55
  165.2 0.6 add_compare_fusion.5
  165.8 1.4 fusion.54
  167.6 1.5 fusion.55
  169.2 0.6 add_compare_fusion.5
  169.8 1.4 fusion.54
  171.7 1.5 fusion.55
  173.3 0.6 add_compare_fusion.5
  173.8 1.4 fusion.54
  175.7 1.5 fusion.55
  177.3 0.6 add_compare_fusion.5
  177.9 1.4 fusion.54
  179.8 1.5 fusion.55
  181.4 0.6 add_compare_fusion.5
  181.9 1.4 fusion.54
  183.8 1.5 fusion.55
  185.4 0.6 add_compare_fusion.5
  186.0 1.4 fusion.54
  187.9 1.5 fusion.55
  189.5 32.3 %while.31 = (s32[]{:T(128)}, f32[8,256]{1,0:T(8,128)S(1)}, f32[8,256]{1,0:T(8,128)S(1)}, f32[8,256,64]{1,2,0:T(8,128)S(1)}, bf16[8,256,64]{2,1,0:T(8,128)(2,1)S(...) while((s32[]{:T(128)}, f32[8,256]{1,0:T(8,128)S(1)}, ...), condition=%wide.region_10.11_spmd.clone, body=%wide.region_7.10_spmd.clone.sunk | while | flops 138415616 | bytes 6961285 | solution.py:32
  189.5 0.6 add_compare_fusion.6
  190.1 1.4 fusion.57
  192.0 1.5 fusion.58
  193.6 0.6 add_compare_fusion.6
  194.1 1.4 fusion.57
  196.0 1.5 fusion.58
  197.6 0.6 add_compare_fusion.6
  198.2 1.4 fusion.57
  200.1 1.5 fusion.58
  201.7 0.6 add_compare_fusion.6
  202.2 1.4 fusion.57
  204.1 1.5 fusion.58
  205.7 0.6 add_compare_fusion.6
  206.3 1.4 fusion.57
  208.2 1.5 fusion.58
  210.3 1.4 fusion.57
  212.2 1.5 fusion.58
  214.4 1.4 fusion.57
  216.2 1.5 fusion.58
  218.4 1.4 fusion.57
  220.3 1.5 fusion.58
  222.0 0.8 fusion.32
  222.8 41.9 %all-gather.8.cloned.1.call-done = bf16[256,4096]{0,1:T(8,128)(2,1)} async-done(((bf16[256,512]{0,1:T(8,128)(2,1)}), bf16[256,4096]{0,1:T(8,128)(2,1)}) %all-gather.8.cloned.1.call-update) | async-done | bytes 2097168 | tf_op jit(solution)/shard_map/all_gather | solution.py:81
  264.7 4.8 %convolution_convert_fusion = bf16[256,512]{1,0:T(8,128)(2,1)} fusion(bf16[256,4096]{0,1:T(8,128)(2,1)} %all-gather.8.cloned.1.call-done, bf16[4096,512]{1,0:T(8,128)(2,1)} %bitcast.18), kind=kOutput, calls=%fused_computation.39 | convolution fusion | flops 1073872896 | bytes 6553600 | tf_op jit(solution)/shard_map/dot_general | solution.py:83
  (82 shorter events, 11.4 us)
Async XLA Ops:
  6.5 51.1 %all-gather.4.cloned.1.call-start = ((), (), s32[]{:S(2)}) async-start(), calls=%async_computation.1 | async-start | bytes 2359296 | tf_op jit(solution)/shard_map/all_gather | solution.py:60
  7.3 145.8 %all-gather.6.cloned.1.call-start = ((), (), s32[]{:S(2)}) async-start(), calls=%async_computation.2 | async-start | bytes 4259840 | tf_op jit(solution)/shard_map/all_gather | solution.py:69
  8.0 6.2 %copy-start = (bf16[2048,512]{1,0:T(8,128)(2,1)S(1)}, bf16[2048,512]{1,0:T(8,128)(2,1)}, u32[]{:S(2)}) copy-start(bf16[2048,512]{1,0:T(8,128)(2,1)} %param.15) | copy-start | bytes 6291460
  12.1 6.9 %copy-start.2 = (bf16[64,512]{1,0:T(8,128)(2,1)S(1)}, bf16[64,512]{1,0:T(8,128)(2,1)}, u32[]{:S(2)}) copy-start(bf16[64,512]{1,0:T(8,128)(2,1)} %param.17) | copy-start | bytes 196612
  12.1 177.3 %collective-permute-start.1 = (bf16[2048,512]{0,1:T(8,128)(2,1)}, bf16[2048,512]{0,1:T(8,128)(2,1)}, u32[]{:S(2)}, u32[]{:S(2)}) collective-permute-start(bf16[2048,512]{0,1:T(8,128)(2,1)} %copy.12), channel_id=1, source_target_pairs={{0,8},{8,0},{16,24},{24,16},{32,40},{40,32},{48,56},{56,48},{64,72... | collective-permute-start | bytes 6291464 | tf_op jit(solution)/shard_map/ppermute | solution.py:12
  16.6 172.8 %collective-permute-start = (bf16[2048,512]{0,1:T(8,128)(2,1)}, bf16[2048,512]{0,1:T(8,128)(2,1)}, u32[]{:S(2)}, u32[]{:S(2)}) collective-permute-start(bf16[2048,512]{0,1:T(8,128)(2,1)} %copy.11), channel_id=1, source_target_pairs={{0,8},{8,0},{16,24},{24,16},{32,40},{40,32},{48,56},{56,48},{64,72... | collective-permute-start | bytes 6291464 | tf_op jit(solution)/shard_map/ppermute | solution.py:12
  21.5 14.3 %copy-start.4 = (s32[32]{0:T(128)S(1)}, s32[32]{0:T(128)}, u32[]{:S(2)}) copy-start(s32[32]{0:T(128)} %param.18) | copy-start | bytes 388
  21.5 15.5 %copy-start.5 = (s32[32]{0:T(128)S(1)}, s32[32]{0:T(128)}, u32[]{:S(2)}) copy-start(s32[32]{0:T(128)} %param.19) | copy-start | bytes 388
  21.5 201.2 %all-to-all-start = ((bf16[64,64,512]{2,1,0:T(8,128)(2,1)}), bf16[64,64,512]{2,1,0:T(8,128)(2,1)}, u32[]{:S(2)}, u32[]{:S(2)}) async-start(bf16[64,64,512]{2,1,0:T(8,128)(2,1)} %stack.2), calls=%async_computation | async-start | bytes 8388608 | tf_op jit(solution)/shard_map/all_to_all | solution.py:86
  35.7 117.3 %copy-start.3 = (f32[4096]{0:T(1024)S(1)}, f32[4096]{0:T(1024)}, u32[]{:S(2)}) copy-start(f32[4096]{0:T(1024)} %param.13) | copy-start | bytes 49156
  35.7 229.0 %all-gather.8.cloned.1.call-start = ((), (), s32[]{:S(2)}) async-start(), calls=%async_computation.3 | async-start | bytes 2359296 | tf_op jit(solution)/shard_map/all_gather | solution.py:81
  57.7 95.4 %copy-start.1 = (bf16[256,4096]{1,0:T(8,128)(2,1)S(1)}, bf16[256,4096]{1,0:T(8,128)(2,1)}, u32[]{:S(2)}) copy-start(bf16[256,4096]{1,0:T(8,128)(2,1)} %all-gather.4.cloned.1.call-done) | copy-start | bytes 6291460
Sparse Core Ops, SparseCore 0:
  9.4 48.1 all-gather.3
  61.0 91.9 all-gather.5
  222.9 41.7 all-gather.7
